TPU v7x, 256 devices: a whole 4x4x8 slice. The times are simulated.
256 devices in a mesh: batch: 4 (over x_hi, core), hidden: 16 (over x_lo, z), width: 4 (over y).
Axes of the slice: x: 4 (x_hi: 2, x_lo: 2; x = x_hi * 2 + x_lo), y: 4, z: 8, core: 2. Of those that a mesh axis runs over, the one named last changes fastest.
Arguments:
- frames: bfloat16 [4, 512, 1280], P('batch', None, 'hidden'), may hold values from -6 to 6
- adapter_weight: bfloat16 [4, 1280, 16384], P(None, 'hidden', 'width'), may hold values from -0.078125 to 0.078125
- text_embed: bfloat16 [512, 16384], P('batch', 'width'), may hold values from -6 to 6
- audio_len: int32 [4], P('batch'), may hold values from 16 to 64, as said below
- text_len: int32 [4], P('batch'), may hold values from 32 to 112, as said below
- norm_gain: bfloat16 [16384], P('width'), may hold values from 0.5 to 1.5
- gate_up: bfloat16 [16384, 2, 26624], P('width', None, ('batch', 'hidden')), may hold values from -0.046875 to 0.046875
- cotangent: bfloat16 [512, 26624], P('width', ('batch', 'hidden')), may hold values from -0.59765625 to 0.59765625
Outputs:
- hidden: bfloat16 [512, 26624], P('width', ('batch', 'hidden'))
- weight_grad: float32 [4, 1280, 16384], P(None, 'hidden', 'width')
Inputs may be any that keep to these rules, and one draw needn't show every extreme that they name: `audio_len`: some sequence holds exactly 16 audio positions and another exactly 64. audio_len + text_len never exceeds 128, and equals it in some sequence.
All inputs are finite; a program needn't handle non-finite values.
Results may differ from a plain program's by a relative error of at most 0.0059.
Values may be sent and summed in bfloat16 or wider, within the bound.
A program may use at most 64 MiB of HBM per device.

v0:
```python
import jax
import jax.numpy as jnp
from jax import lax
from jax.sharding import PartitionSpec as P

D = 16384
HEAD = 64
norm_eps = 1e-05


def on_device(
    frames, adapter_weight, text_embed, audio_len, text_len, norm_gain, gate_up, cotangent
):
    feat_here = frames.shape[2]
    seq_len = frames.shape[1] // 4
    width_here = adapter_weight.shape[2]
    stacked = frames[0, : 4 * HEAD].reshape(HEAD, 4 * feat_here)
    kernel = adapter_weight.reshape(4 * feat_here, width_here)
    partial_audio = jnp.dot(stacked, kernel, preferred_element_type=jnp.float32)
    audio_part = lax.psum(partial_audio, "hidden")
    positions = jnp.arange(seq_len, dtype=jnp.int32)
    is_audio = positions < audio_len[0]
    is_text = jnp.logical_and(jnp.logical_not(is_audio), positions < audio_len[0] + text_len[0])
    text_vals = jnp.where(is_text[:, None], text_embed.astype(jnp.float32), 0.0)
    stream = jnp.concatenate(
        [jnp.where(is_audio[:HEAD, None], audio_part, text_vals[:HEAD]), text_vals[HEAD:]], axis=0
    )
    gain_vals = norm_gain.astype(jnp.float32)
    sum_squares = lax.psum(jnp.sum(stream * stream, axis=1), "width")
    inv_rms = lax.rsqrt(sum_squares / D + norm_eps)
    normed = (stream * inv_rms[:, None] * gain_vals[None, :]).astype(jnp.bfloat16)
    masked = jnp.where(is_audio[:HEAD, None], stacked, jnp.zeros_like(stacked))
    all_stacked = lax.all_gather(masked, "batch", axis=0, tiled=True)
    all_inv = lax.all_gather(inv_rms[:HEAD], "batch", axis=0, tiled=True)
    all_normed = lax.all_gather(normed, "batch", axis=0, tiled=True)
    weights = gate_up.reshape(width_here, -1)
    half = weights.shape[1] // 2
    partial_pair = jnp.dot(all_normed, weights, preferred_element_type=jnp.float32)
    summed = lax.psum_scatter(partial_pair, "width", scatter_dimension=0, tiled=True)
    gate_vals = summed[:, :half]
    up_vals = summed[:, half:]
    sigmoid_gate = jax.nn.sigmoid(gate_vals)
    silu_gate = gate_vals * sigmoid_gate
    hidden = (silu_gate * up_vals).astype(jnp.bfloat16)
    cot_vals = cotangent[:HEAD].astype(jnp.float32)
    gate_head, up_head, sig_head = (gate_vals[:HEAD], up_vals[:HEAD], sigmoid_gate[:HEAD])
    grad_gate = cot_vals * up_head * sig_head * (1.0 + gate_head * (1.0 - sig_head))
    grad_up = cot_vals * silu_gate[:HEAD]
    inner = jnp.sum(grad_gate * gate_head + grad_up * up_head, axis=1) / D
    grad_pair = jnp.concatenate([grad_gate, grad_up], axis=1).astype(jnp.bfloat16)
    all_pairs = lax.all_gather(grad_pair, "width", axis=0, tiled=True)
    all_inner = lax.all_gather(inner, "width", axis=0, tiled=True)
    partial = lax.dot_general(
        all_pairs, weights, (((1,), (1,)), ((), ())), preferred_element_type=jnp.float32
    )
    head_normed = all_normed.reshape(-1, seq_len, width_here)[:, :HEAD].reshape(-1, width_here)
    head_unit = head_normed.astype(jnp.float32) / gain_vals[None, :]
    share = (gain_vals[None, :] * partial - head_unit * all_inner[:, None]) * all_inv[:, None]
    grad_share = lax.psum_scatter(share, ("batch", "hidden"), scatter_dimension=0, tiled=True)
    audio_grad = lax.all_gather(
        grad_share.astype(jnp.bfloat16), ("batch", "hidden"), axis=0, tiled=True
    )
    weight_grad = lax.dot_general(
        all_stacked, audio_grad, (((0,), (0,)), ((), ())), preferred_element_type=jnp.float32
    )
    return (hidden, weight_grad.reshape(4, feat_here, width_here))


def solution(mesh):
    return jax.shard_map(
        on_device,
        mesh=mesh,
        in_specs=(
            P("batch", None, "hidden"),
            P(None, "hidden", "width"),
            P("batch", "width"),
            P("batch"),
            P("batch"),
            P("width"),
            P("width", None, ("batch", "hidden")),
            P("width", ("batch", "hidden")),
        ),
        out_specs=(P("width", ("batch", "hidden")), P(None, "hidden", "width")),
        check_vma=False,
    )
```

profile of v0, /device:TPU:99, one launch (start us, length us, event | category | flops | bytes accessed | tf_op | source)
XLA Modules:
  0.0 773.7 jit_solution(12971479772562971977)
XLA Ops:
  7.2 0.0 copy-start
  7.2 0.0 copy-start.4
  7.2 0.0 all-reduce.6.cloned.1.call-start
  7.2 0.9 slice.43
  8.2 0.1 copy.11
  8.3 0.1 reshape_squeeze.3
  8.4 0.5 copy-done
  8.9 1.7 fusion.9
  10.6 0.0 all-reduce.6.cloned.1.call-update
  10.6 0.0 all-gather.4.cloned.1.call-start
  12.0 0.0 copy-done.4
  12.0 2.8 convert_select_fusion
  14.8 121.5 %all-reduce.6.cloned.1.call-done = f32[64,4096]{1,0:T(8,128)} async-done(((f32[64,4096]{1,0:T(8,128)}), f32[64,4096]{1,0:T(8,128)}) %all-reduce.6.cloned.1.call-update) | async-done | bytes 1048592 | tf_op jit(solution)/shard_map/psum | solution.py:20
  136.3 2.1 slice_select_fusion
  138.4 0.0 copy-start.1
  138.4 0.0 copy-start.2
  138.4 1.0 copy-done.1
  139.4 0.3 copy-done.2
  139.7 0.2 multiply_reduce_fusion
  139.9 8.8 %psum.15 = f32[128]{0:T(128)S(1)} all-reduce(f32[128]{0:T(128)S(1)} %multiply_reduce_fusion), channel_id=1, replica_groups=mesh['batch'=4,'hidden'=16,'width'=4] {'width'}, use_global_device_ids=true, to_apply=%region_2.3 | all-reduce | flops 128 | bytes 1024 | tf_op jit(solution)/shard_map/psum | solution.py:29
  148.8 2.8 multiply_convert_fusion
  151.6 0.0 all-gather.4.cloned.1.call-update
  151.6 0.0 reduce-scatter.2.cloned.1.call-start
  151.7 51.2 %all-gather.4.cloned.1.call-done = bf16[512,4096]{1,0:T(8,128)(2,1)} async-done(((bf16[128,4096]{1,0:T(8,128)(2,1)}), bf16[512,4096]{1,0:T(8,128)(2,1)}) %all-gather.4.cloned.1.call-update) | async-done | bytes 4194320 | tf_op jit(solution)/shard_map/all_gather | solution.py:35
  202.9 0.0 copy-start.7
  202.9 0.0 copy-start.6
  202.9 0.0 copy-start.5
  202.9 9.1 %fusion.10 = f32[512,832]{0,1:T(8,128)} fusion(bf16[512,4096]{1,0:T(8,128)(2,1)} %all-gather.4.cloned.1.call-done, bf16[4096,832]{0,1:T(8,128)(2,1)} %bitcast.32), kind=kOutput, calls=%fused_computation.30 | convolution fusion | flops 3489660928 | bytes 12713984 | tf_op jit(solution)/shard_map/dot_general | solution.py:38
  212.1 0.0 reduce-scatter.2.cloned.1.call-update
  212.1 0.0 copy-start.3
  212.1 0.0 all-gather.6.cloned.1.call-start
  212.2 0.0 copy-done.7
  212.2 0.6 dynamic-slice
  212.8 0.0 copy-done.6
  212.8 0.6 dynamic-slice.1
  214.7 0.0 copy-done.5
  214.7 0.6 dynamic-slice.2
  215.9 0.1 slice_dynamic-update-slice_fusion
  216.0 6.8 all-reduce.1
  222.8 3.4 slice.63
  226.2 15.0 %reduce-scatter.2.cloned.1.call-done = f32[128,832]{0,1:T(8,128)} async-done(((f32[512,832]{0,1:T(8,128)}), f32[128,832]{0,1:T(8,128)}) %reduce-scatter.2.cloned.1.call-update) | async-done | bytes 426000 | tf_op jit(solution)/shard_map/reduce_scatter | solution.py:39
  241.2 1.7 add_divide_fusion
  242.9 0.0 copy-done.3
  242.9 1.2 add_reduce_fusion
  244.2 0.1 copy.12
  244.3 9.8 %all_gather.20 = bf16[256,832]{1,0:T(8,128)(2,1)S(1)} all-gather(bf16[64,832]{1,0:T(8,128)(2,1)S(1)} %copy.12), channel_id=1, replica_groups=mesh['batch'=4,'hidden'=16,'width'=4] {'width'}, dimensions={0}, use_global_device_ids=true | all-gather | bytes 532480 | tf_op jit(solution)/shard_map/all_gather | solution.py:51
  254.1 0.1 multiply_dynamic-update-slice_fusion
  254.2 7.6 all-reduce
  261.7 8.1 %fusion.1 = f32[256,4096]{1,0:T(8,128)} fusion(bf16[256,832]{1,0:T(8,128)(2,1)S(1)} %all_gather.20, bf16[4096,832]{0,1:T(8,128)(2,1)} %bitcast.33, bf16[256,4096]{1,0:T(8,128)(2,1)} %bitcast.28, f32[256]{0:T(256)S(1)} %all-reduce.1, f32[256]{0:T(256)S(1)} %all-reduce, f32[4096]{0:T(1024)S(1)} %convert_element_type.26), kind=kOutput, calls=%fused_computation.2 | convolution fusion | flops 1751121920 | bytes 13551616 | tf_op jit(solution)/shard_map/dot_general | solution.py:53
  269.8 281.6 %all-reduce.7 = bf16[256,4096]{1,0:T(8,128)(2,1)} all-reduce(f32[256,4096]{1,0:T(8,128)} %fusion.1), channel_id=3, replica_groups=mesh['batch'=4,'hidden'=16,'width'=4] {'batch','hidden'}, use_global_device_ids=true, to_apply=%region_5.6.clone | all-reduce | flops 1048576 | bytes 6291456
  551.4 1.5 fusion.7
  552.9 0.0 all-gather.6.cloned.1.call-update
  552.9 0.1 broadcast_select_fusion
  553.0 17.8 %all_gather.19 = bf16[256,320]{1,0:T(8,128)(2,1)S(1)} all-gather(bf16[64,320]{1,0:T(8,128)(2,1)S(1)} %broadcast_select_fusion), channel_id=1, replica_groups=mesh['batch'=4,'hidden'=16,'width'=4] {'batch'}, dimensions={0}, use_global_device_ids=true | all-gather | bytes 204800 | tf_op jit(solution)/shard_map/all_gather | solution.py:33
  570.8 187.6 %all-gather.6.cloned.1.call-done = bf16[64,4,4096]{2,1,0:T(4,128)(2,1)} async-done(((bf16[1,4,4096]{2,1,0:T(4,128)(2,1)}), bf16[64,4,4096]{2,1,0:T(4,128)(2,1)}) %all-gather.6.cloned.1.call-update) | async-done | bytes 2097168 | tf_op jit(solution)/shard_map/all_gather | solution.py:60
  758.4 4.0 reshape.44
  762.4 4.8 fusion.11
  (7 shorter events, 0.1 us)
Async XLA Ops:
  7.2 1.8 copy-start
  7.2 4.8 copy-start.4
  7.2 129.1 %all-reduce.6.cloned.1.call-start = ((), (), s32[]{:S(2)}) async-start(), calls=%async_computation.1 | async-start | bytes 2097152 | tf_op jit(solution)/shard_map/psum | solution.py:20
  10.6 192.3 %all-gather.4.cloned.1.call-start = ((), (), s32[]{:S(2)}) async-start(), calls=%async_computation.2 | async-start | bytes 5242880 | tf_op jit(solution)/shard_map/all_gather | solution.py:35
  138.4 1.0 copy-start.1
  138.4 1.3 copy-start.2
  151.6 89.6 %reduce-scatter.2.cloned.1.call-start = ((), (), s32[]{:S(2)}) async-start(), calls=%async_computation.3 | async-start | bytes 2129920 | tf_op jit(solution)/shard_map/reduce_scatter | solution.py:39
  202.9 9.2 %copy-start.7 = (u32[256]{0:T(256)S(1)}, u32[256]{0:T(256)}, u32[]{:S(2)}) copy-start(u32[256]{0:T(256)} %constant.21) | copy-start | bytes 3076
  202.9 9.9 %copy-start.6 = (u32[256]{0:T(256)S(1)}, u32[256]{0:T(256)}, u32[]{:S(2)}) copy-start(u32[256]{0:T(256)} %constant.26) | copy-start | bytes 3076
  202.9 11.8 %copy-start.5 = (u32[256]{0:T(256)S(1)}, u32[256]{0:T(256)}, u32[]{:S(2)}) copy-start(u32[256]{0:T(256)} %constant.33) | copy-start | bytes 3076
  212.1 30.9 %copy-start.3 = (bf16[128,416]{0,1:T(8,128)(2,1)S(1)}, bf16[128,416]{0,1:T(8,128)(2,1)}, u32[]{:S(2)}) copy-start(bf16[128,416]{0,1:T(8,128)(2,1)} %param.15) | copy-start | bytes 319492
  212.1 546.3 %all-gather.6.cloned.1.call-start = ((), (), s32[]{:S(2)}) async-start(), calls=%async_computation.4 | async-start | bytes 2129920 | tf_op jit(solution)/shard_map/all_gather | solution.py:60
Sparse Core Ops, SparseCore 0:
  10.8 125.5 all-reduce.5
  151.7 51.1 all-gather.3
  212.2 28.9 reduce-scatter.1
  553.1 205.2 all-gather.5
where the time goes:
time: 774 us
  waiting for transfers between devices  375 us (48%)
  blocking collectives  332 us (43%)
  matrix products  23.7 us (3%)
  between operations  17.1 us (2%)
  local copies, waits for them, and re-layouts  13.9 us (2%)
  other arithmetic  11.1 us (1%)
    unnamed x3, blocking collectives  296 us
    all_gather x1, waiting for transfers between devices, on_device(): lax.all_gather(grad_share.astype(jnp.bfloat16), ('batch', 'hidden'), axis...  188 us
    psum x1, waiting for transfers between devices, on_device(): audio_part = lax.psum(partial_audio, 'hidden')  121 us
    all_gather x1, waiting for transfers between devices, on_device(): all_normed = lax.all_gather(normed, 'batch', axis=0, tiled=True)  51.2 us
    all_gather x1, blocking collectives, on_device(): all_stacked = lax.all_gather(masked, 'batch', axis=0, tiled=True)  17.8 us
  transfers between devices with their start and end apart: 4, of which 4 were waited for; matrix products, arithmetic and copies ran while one was open for 1% of the time, Pallas kernels for 0%

commit v1 on v0

--- a/solution.py
+++ b/solution.py
@@ -57,8 +57,14 @@
     head_unit = head_normed.astype(jnp.float32) / gain_vals[None, :]
     share = (gain_vals[None, :] * partial - head_unit * all_inner[:, None]) * all_inv[:, None]
     grad_share = lax.psum_scatter(share, ("batch", "hidden"), scatter_dimension=0, tiled=True)
-    audio_grad = lax.all_gather(
-        grad_share.astype(jnp.bfloat16), ("batch", "hidden"), axis=0, tiled=True
+    audio_grad = jnp.concatenate(
+        lax.all_to_all(
+            jnp.stack([grad_share.astype(jnp.bfloat16)] * lax.axis_size(("batch", "hidden"))),
+            ("batch", "hidden"),
+            0,
+            0,
+        ),
+        axis=0,
     )
     weight_grad = lax.dot_general(
         all_stacked, audio_grad, (((0,), (0,)), ((), ())), preferred_element_type=jnp.float32

time: 774 us -> 654 us (0.84)
  waiting for transfers between devices: 375 us -> 224 us
  starting transfers between devices: 0.16 us -> 29.6 us
    all_gather x1 -> x0, waiting for transfers between devices: 188 us -> none  [on_device(): lax.all_gather(grad_share.astype(jnp.bfloat16), ('batch', 'hidden'), axis...]
    all_to_all x0 -> x1, waiting for transfers between devices: none -> 36.1 us  [on_device(): lax.all_to_all(jnp.stack([grad_share.astype(jnp.bfloat16)] * lax.axis_siz...]
    all_to_all x0 -> x1, starting transfers between devices: none -> 29.5 us  [on_device(): lax.all_to_all(jnp.stack([grad_share.astype(jnp.bfloat16)] * lax.axis_siz...]
where the time goes in v1:
time: 654 us; the launch traced here: 649 us
  blocking collectives  328 us (50%)
  waiting for transfers between devices  224 us (34%)
  starting transfers between devices  29.6 us (5%)
  matrix products  23.7 us (4%)
  between operations  17.1 us (3%)
  local copies, waits for them, and re-layouts  15.7 us (2%)
  other arithmetic  11.1 us (2%)
    unnamed x3, blocking collectives  296 us
    psum x1, waiting for transfers between devices, on_device(): audio_part = lax.psum(partial_audio, 'hidden')  121 us
    all_gather x1, waiting for transfers between devices, on_device(): all_normed = lax.all_gather(normed, 'batch', axis=0, tiled=True)  51.2 us
    all_to_all x1, waiting for transfers between devices, on_device(): lax.all_to_all(jnp.stack([grad_share.astype(jnp.bfloat16)] * lax.axis_siz...  36.1 us
    all_to_all x1, starting transfers between devices, on_device(): lax.all_to_all(jnp.stack([grad_share.astype(jnp.bfloat16)] * lax.axis_siz...  29.5 us
    reduce_scatter x1, waiting for transfers between devices, on_device(): lax.psum_scatter(partial_pair, 'width', scatter_dimension=0, tiled=True)  15.1 us
  transfers between devices with their start and end apart: 4, of which 4 were waited for; matrix products, arithmetic and copies ran while one was open for 1% of the time, Pallas kernels for 0%

profile of v1, /device:TPU:99, one launch (start us, length us, event | category | flops | bytes accessed | tf_op | source)
XLA Modules:
  0.0 648.8 jit_solution(13225152780866141676)
XLA Ops:
  7.2 0.0 copy-start
  7.2 0.0 copy-start.4
  7.2 0.0 all-reduce.6.cloned.1.call-start
  7.2 0.9 slice.43
  8.2 0.1 copy.12
  8.3 0.1 reshape_squeeze.3
  8.4 0.5 copy-done
  8.9 1.7 fusion.8
  10.6 0.0 all-reduce.6.cloned.1.call-update
  10.6 0.0 all-gather.2.cloned.1.call-start
  12.0 0.0 copy-done.4
  12.0 2.8 convert_select_fusion
  14.8 121.5 %all-reduce.6.cloned.1.call-done = f32[64,4096]{1,0:T(8,128)} async-done(((f32[64,4096]{1,0:T(8,128)}), f32[64,4096]{1,0:T(8,128)}) %all-reduce.6.cloned.1.call-update) | async-done | bytes 1048592 | tf_op jit(solution)/shard_map/psum | solution.py:20
  136.3 2.1 slice_select_fusion
  138.4 0.0 copy-start.1
  138.4 0.0 copy-start.2
  138.4 1.0 copy-done.1
  139.4 0.3 copy-done.2
  139.7 0.2 multiply_reduce_fusion
  139.9 8.8 %psum.15 = f32[128]{0:T(128)S(1)} all-reduce(f32[128]{0:T(128)S(1)} %multiply_reduce_fusion), channel_id=1, replica_groups=mesh['batch'=4,'hidden'=16,'width'=4] {'width'}, use_global_device_ids=true, to_apply=%region_2.3 | all-reduce | flops 128 | bytes 1024 | tf_op jit(solution)/shard_map/psum | solution.py:29
  148.8 2.8 multiply_convert_fusion
  151.6 0.0 all-gather.2.cloned.1.call-update
  151.6 0.0 reduce-scatter.2.cloned.1.call-start
  151.7 51.2 %all-gather.2.cloned.1.call-done = bf16[512,4096]{1,0:T(8,128)(2,1)} async-done(((bf16[128,4096]{1,0:T(8,128)(2,1)}), bf16[512,4096]{1,0:T(8,128)(2,1)}) %all-gather.2.cloned.1.call-update) | async-done | bytes 4194320 | tf_op jit(solution)/shard_map/all_gather | solution.py:35
  202.9 0.0 copy-start.7
  202.9 0.0 copy-start.6
  202.9 0.0 copy-start.5
  202.9 9.1 %fusion.9 = f32[512,832]{0,1:T(8,128)} fusion(bf16[512,4096]{1,0:T(8,128)(2,1)} %all-gather.2.cloned.1.call-done, bf16[4096,832]{0,1:T(8,128)(2,1)} %bitcast.32), kind=kOutput, calls=%fused_computation.29 | convolution fusion | flops 3489660928 | bytes 12713984 | tf_op jit(solution)/shard_map/dot_general | solution.py:38
  212.1 0.0 reduce-scatter.2.cloned.1.call-update
  212.1 0.0 copy-start.3
  212.1 0.0 copy-done.7
  212.1 0.6 dynamic-slice
  212.7 0.0 copy-done.6
  212.7 0.6 dynamic-slice.1
  214.6 0.0 copy-done.5
  214.6 0.6 dynamic-slice.2
  215.9 0.1 slice_dynamic-update-slice_fusion
  216.0 6.8 %all-reduce.1 = f32[256]{0:T(256)S(1)} all-reduce(f32[256]{0:T(256)S(1)} %slice_dynamic-update-slice_fusion), channel_id=1, replica_groups=mesh['batch'=4,'hidden'=16,'width'=4] {'batch'}, use_global_device_ids=true, to_apply=%add.1 | all-reduce | flops 256 | bytes 2048
  222.7 3.4 slice.63
  226.1 15.1 %reduce-scatter.2.cloned.1.call-done = f32[128,832]{0,1:T(8,128)} async-done(((f32[512,832]{0,1:T(8,128)}), f32[128,832]{0,1:T(8,128)}) %reduce-scatter.2.cloned.1.call-update) | async-done | bytes 426000 | tf_op jit(solution)/shard_map/reduce_scatter | solution.py:39
  241.2 1.7 add_divide_fusion
  242.9 0.0 copy-done.3
  242.9 1.2 add_reduce_fusion
  244.2 0.1 copy.14
  244.3 9.8 %all_gather.17 = bf16[256,832]{1,0:T(8,128)(2,1)S(1)} all-gather(bf16[64,832]{1,0:T(8,128)(2,1)S(1)} %copy.14), channel_id=1, replica_groups=mesh['batch'=4,'hidden'=16,'width'=4] {'width'}, dimensions={0}, use_global_device_ids=true | all-gather | bytes 532480 | tf_op jit(solution)/shard_map/all_gather | solution.py:51
  254.1 0.1 multiply_dynamic-update-slice_fusion
  254.2 7.6 %all-reduce = f32[256]{0:T(256)S(1)} all-reduce(f32[256]{0:T(256)S(1)} %multiply_dynamic-update-slice_fusion), channel_id=1, replica_groups=mesh['batch'=4,'hidden'=16,'width'=4] {'width'}, use_global_device_ids=true, to_apply=%add | all-reduce | flops 256 | bytes 2048
  261.7 8.1 %fusion.1 = f32[256,4096]{1,0:T(8,128)} fusion(bf16[256,832]{1,0:T(8,128)(2,1)S(1)} %all_gather.17, bf16[4096,832]{0,1:T(8,128)(2,1)} %bitcast.33, bf16[256,4096]{1,0:T(8,128)(2,1)} %bitcast.26, f32[256]{0:T(256)S(1)} %all-reduce.1, f32[256]{0:T(256)S(1)} %all-reduce, f32[4096]{0:T(1024)S(1)} %convert_element_type.26), kind=kOutput, calls=%fused_computation.2 | convolution fusion | flops 1751121920 | bytes 13551616 | tf_op jit(solution)/shard_map/dot_general | solution.py:53
  269.8 281.6 %all-reduce.7 = bf16[256,4096]{1,0:T(8,128)(2,1)} all-reduce(f32[256,4096]{1,0:T(8,128)} %fusion.1), channel_id=3, replica_groups=mesh['batch'=4,'hidden'=16,'width'=4] {'batch','hidden'}, use_global_device_ids=true, to_apply=%region_5.6.clone | all-reduce | flops 1048576 | bytes 6291456
  551.4 0.9 dynamic-slice_convert_fusion
  552.3 2.3 stack.2
  554.6 29.5 %all-to-all-start = ((bf16[64,4,4096]{2,1,0:T(4,128)(2,1)}), bf16[64,4,4096]{2,1,0:T(4,128)(2,1)}, u32[]{:S(2)}, u32[]{:S(2)}) async-start(bf16[64,4,4096]{2,1,0:T(4,128)(2,1)} %stack.2), calls=%async_computation.1 | async-start | bytes 4194304 | tf_op jit(solution)/shard_map/all_to_all | solution.py:61
  584.1 0.1 broadcast_select_fusion
  584.2 13.0 %all_gather.16 = bf16[256,320]{1,0:T(8,128)(2,1)S(1)} all-gather(bf16[64,320]{1,0:T(8,128)(2,1)S(1)} %broadcast_select_fusion), channel_id=1, replica_groups=mesh['batch'=4,'hidden'=16,'width'=4] {'batch'}, dimensions={0}, use_global_device_ids=true | all-gather | bytes 204800 | tf_op jit(solution)/shard_map/all_gather | solution.py:33
  597.3 0.1 copy.13
  597.4 36.1 %all-to-all-done = bf16[64,4,4096]{2,1,0:T(4,128)(2,1)} async-done(((bf16[64,4,4096]{2,1,0:T(4,128)(2,1)}), bf16[64,4,4096]{2,1,0:T(4,128)(2,1)}, u32[]{:S(2)}, u32[]{:S(2)}) %all-to-all-start) | async-done | bytes 2097184 | tf_op jit(solution)/shard_map/all_to_all | solution.py:61
  633.5 4.0 reshape.51
  637.5 4.8 fusion.10
  (7 shorter events, 0.1 us)
Async XLA Ops:
  7.2 1.8 copy-start
  7.2 4.8 copy-start.4
  7.2 129.1 %all-reduce.6.cloned.1.call-start = ((), (), s32[]{:S(2)}) async-start(), calls=%async_computation.2 | async-start | bytes 2097152 | tf_op jit(solution)/shard_map/psum | solution.py:20
  10.6 192.3 %all-gather.2.cloned.1.call-start = ((), (), s32[]{:S(2)}) async-start(), calls=%async_computation.3 | async-start | bytes 5242880 | tf_op jit(solution)/shard_map/all_gather | solution.py:35
  138.4 1.0 copy-start.1
  138.4 1.3 copy-start.2
  151.6 89.6 %reduce-scatter.2.cloned.1.call-start = ((), (), s32[]{:S(2)}) async-start(), calls=%async_computation.4 | async-start | bytes 2129920 | tf_op jit(solution)/shard_map/reduce_scatter | solution.py:39
  202.9 9.2 %copy-start.7 = (u32[256]{0:T(256)S(1)}, u32[256]{0:T(256)}, u32[]{:S(2)}) copy-start(u32[256]{0:T(256)} %constant.21) | copy-start | bytes 3076
  202.9 9.8 %copy-start.6 = (u32[256]{0:T(256)S(1)}, u32[256]{0:T(256)}, u32[]{:S(2)}) copy-start(u32[256]{0:T(256)} %constant.26) | copy-start | bytes 3076
  202.9 11.7 %copy-start.5 = (u32[256]{0:T(256)S(1)}, u32[256]{0:T(256)}, u32[]{:S(2)}) copy-start(u32[256]{0:T(256)} %constant.33) | copy-start | bytes 3076
  212.1 30.9 %copy-start.3 = (bf16[128,416]{0,1:T(8,128)(2,1)S(1)}, bf16[128,416]{0,1:T(8,128)(2,1)}, u32[]{:S(2)}) copy-start(bf16[128,416]{0,1:T(8,128)(2,1)} %param.15) | copy-start | bytes 319492
  554.6 78.9 %all-to-all-start = ((bf16[64,4,4096]{2,1,0:T(4,128)(2,1)}), bf16[64,4,4096]{2,1,0:T(4,128)(2,1)}, u32[]{:S(2)}, u32[]{:S(2)}) async-start(bf16[64,4,4096]{2,1,0:T(4,128)(2,1)} %stack.2), calls=%async_computation.1 | async-start | bytes 4194304 | tf_op jit(solution)/shard_map/all_to_all | solution.py:61
Sparse Core Ops, SparseCore 0:
  10.8 125.5 all-reduce.5
  151.7 51.1 all-gather.1
  212.2 28.9 reduce-scatter.1
